TPU v7x, 32 devices: a whole 2x2x4 slice. The times are simulated.
32 devices in a mesh: dp: 8 (over z, y), mp: 4 (over x, core).
Axes of the slice: x: 2, y: 2, z: 4, core: 2. Of those that a mesh axis runs over, the one named last changes fastest.
Arguments:
- token_pool: bfloat16 [4096, 3072], P('dp'), may hold values from -6 to 6
- visible: int32 [1024], P('dp'), may hold values from 0 to 511, as said below
- out_grad: bfloat16 [1024, 3072], P('dp'), may hold values from -2.5 to 2.5
- ln_gain: float32 [3072], replicated, may hold values from 0.5 to 1.5
- master_up: float32 [3072, 12288], P('dp', 'mp'), may hold values from -0.109375 to 0.109375
- master_down: float32 [3072, 12288], P('dp', 'mp'), may hold values from -0.0546875 to 0.0546875
- row_up: float32 [3072], P('dp'), may hold values from 0.02 to 5
- col_up: float32 [12288], P('mp'), may hold values from 0.05 to 0.5
- row_down: float32 [3072], P('dp'), may hold values from 0.02 to 5
- col_down: float32 [12288], P('mp'), may hold values from 0.05 to 0.5
Outputs:
- update_up: float32 [3072, 12288], P('dp', 'mp')
- update_down: float32 [3072, 12288], P('dp', 'mp')
- row_up_new: float32 [3072], P('dp')
- col_up_new: float32 [12288], P('mp')
- row_down_new: float32 [3072], P('dp')
- col_down_new: float32 [12288], P('mp')
Inputs may be any that keep to these rules, and one draw needn't show every extreme that they name: `visible`: each aligned block of 128 entries lists distinct patch indices of that block's 512 patches, in rising order.
All inputs are finite; a program needn't handle non-finite values.
Results may differ from a plain program's by a relative error of at most 0.0059.
Values may be sent and summed in bfloat16 or wider, within the bound.
A program may use at most 256 MiB of HBM per device.

v0:
```python
import jax
import jax.numpy as jnp
from jax import lax
from jax.sharding import PartitionSpec as P

decay_rate = 0.8
norm_eps = 1e-06
tiny_value = 1e-30


def gelu_tanh(values):
    return jax.nn.gelu(values, approximate=True)


def normalize(values, gain):
    mean_val = jnp.mean(values, axis=1, keepdims=True)
    centred = values - mean_val
    variance = jnp.mean(centred * centred, axis=1, keepdims=True)
    return (centred * lax.rsqrt(variance + norm_eps) * gain).astype(jnp.bfloat16)


def contract_tokens(left, right):
    return lax.dot_general(
        left, right, (((0,), (0,)), ((), ())), preferred_element_type=jnp.float32
    )


def finish_update(grad, row_new, col_new):
    return grad * lax.rsqrt(row_new[:, None] * col_new[None, :])


def on_device(
    token_pool,
    visible,
    out_grad,
    ln_gain,
    master_up,
    master_down,
    row_up,
    col_up,
    row_down,
    col_down,
):
    picked = jnp.take(token_pool, visible, axis=0).astype(jnp.float32)
    normed = normalize(picked, ln_gain)
    grid_rows = master_up.shape[0]
    grid_cols = master_up.shape[1]
    depth = grid_rows * lax.axis_size("dp")
    breadth = grid_cols * lax.axis_size("mp")
    w_up = master_up.astype(jnp.bfloat16)
    w_down = master_down.astype(jnp.bfloat16)
    left = normed
    pre_act = jnp.dot(
        left, lax.all_gather(w_up, "dp", axis=0, tiled=True), preferred_element_type=jnp.float32
    )
    act_value, pull_back = jax.vjp(gelu_tanh, pre_act)
    hidden_act = act_value.astype(jnp.bfloat16)
    left = out_grad
    act_grad = jnp.dot(
        left, lax.all_gather(w_down, "dp", axis=0, tiled=True), preferred_element_type=jnp.float32
    )
    pre_grad = pull_back(act_grad)[0].astype(jnp.bfloat16)
    grad_down = lax.psum_scatter(
        contract_tokens(out_grad, hidden_act), "dp", scatter_dimension=0, tiled=True
    )
    grad_up = lax.psum_scatter(
        contract_tokens(normed, pre_grad), "dp", scatter_dimension=0, tiled=True
    )
    squares_up = grad_up * grad_up + tiny_value
    squares_down = grad_down * grad_down + tiny_value
    rowpart_up = jnp.sum(squares_up, axis=1)
    rowpart_down = jnp.sum(squares_down, axis=1)
    colpart_up = jnp.sum(squares_up, axis=0)
    colpart_down = jnp.sum(squares_down, axis=0)
    rowsum_up, rowsum_down = lax.psum((rowpart_up, rowpart_down), "mp")
    colsum_up, colsum_down = lax.psum((colpart_up, colpart_down), "dp")
    row_up_new = decay_rate * row_up + (1.0 - decay_rate) * rowsum_up / breadth
    row_down_new = decay_rate * row_down + (1.0 - decay_rate) * rowsum_down / breadth
    col_up_new = decay_rate * col_up + (1.0 - decay_rate) * colsum_up / depth
    col_down_new = decay_rate * col_down + (1.0 - decay_rate) * colsum_down / depth
    raw_up = finish_update(grad_up, row_up_new, col_up_new)
    raw_down = finish_update(grad_down, row_down_new, col_down_new)
    energy_up, energy_down = lax.psum(
        (jnp.sum(raw_up * raw_up), jnp.sum(raw_down * raw_down)), ("dp", "mp")
    )
    update_up = raw_up / jnp.maximum(1.0, jnp.sqrt(energy_up / (depth * breadth)))
    update_down = raw_down / jnp.maximum(1.0, jnp.sqrt(energy_down / (depth * breadth)))
    return (update_up, update_down, row_up_new, col_up_new, row_down_new, col_down_new)


def solution(mesh):
    return jax.shard_map(
        on_device,
        mesh=mesh,
        in_specs=(
            P("dp", None),
            P("dp"),
            P("dp", None),
            P(),
            P("dp", "mp"),
            P("dp", "mp"),
            P("dp"),
            P("mp"),
            P("dp"),
            P("mp"),
        ),
        out_specs=(P("dp", "mp"), P("dp", "mp"), P("dp"), P("mp"), P("dp"), P("mp")),
        check_vma=False,
    )
```

profile of v0, /device:TPU:0, one launch (start us, length us, event | category | flops | bytes accessed | tf_op | source)
XLA Modules:
  0.0 2076.0 jit_solution(1462576498393609635)
XLA Ops:
  7.2 4.2 convert_element_type.20
  11.5 4.1 convert_element_type.21
  15.7 0.6 copy-done.15
  16.3 1.9 gather_fusion
  18.2 1.5 convert_reduce_fusion
  19.8 1.6 fusion.8
  21.4 355.3 %all-gather.3.cloned.1.call-done = bf16[3072,3072]{1,0:T(8,128)(2,1)} async-done(((bf16[384,3072]{1,0:T(8,128)(2,1)}), bf16[3072,3072]{1,0:T(8,128)(2,1)}) %all-gather.3.cloned.1.call-update) | async-done | bytes 18874384 | tf_op jit(solution)/shard_map/all_gather | solution.py:60
  376.8 10.1 fusion.43
  386.9 354.4 %all-gather.5.cloned.1.call-done = bf16[3072,3072]{1,0:T(8,128)(2,1)} async-done(((bf16[384,3072]{1,0:T(8,128)(2,1)}), bf16[3072,3072]{1,0:T(8,128)(2,1)}) %all-gather.5.cloned.1.call-update) | async-done | bytes 18874384 | tf_op jit(solution)/shard_map/all_gather | solution.py:54
  741.3 8.0 fusion.41
  749.3 15.0 fusion.18
  764.3 0.2 reduce-scatter.5.cloned.1.call-start
  764.5 15.5 convolution_bitcast_fusion
  780.0 584.0 %reduce-scatter.3.cloned.1.call-done = f32[384,3072]{1,0:T(8,128)} async-done(((f32[3072,3072]{1,0:T(8,128)}), f32[384,3072]{1,0:T(8,128)}) %reduce-scatter.3.cloned.1.call-update) | async-done | bytes 4718608 | tf_op jit(solution)/shard_map/reduce_scatter | solution.py:66
  1364.1 3.2 fusion.1
  1367.3 600.4 %reduce-scatter.5.cloned.1.call-done = f32[384,3072]{1,0:T(8,128)} async-done(((f32[3072,3072]{1,0:T(8,128)}), f32[384,3072]{1,0:T(8,128)}) %reduce-scatter.5.cloned.1.call-update) | async-done | bytes 4718608 | tf_op jit(solution)/shard_map/reduce_scatter | solution.py:63
  1967.7 3.2 fusion.3
  1970.9 6.4 all-reduce.2
  1977.3 35.6 %all-reduce.1 = (f32[3072]{0:T(1024)S(1)}, f32[3072]{0:T(1024)S(1)}) all-reduce(f32[3072]{0:T(1024)S(1)} %get-tuple-element.9, f32[3072]{0:T(1024)S(1)} %get-tuple-element.7), channel_id=1, replica_groups=mesh['dp'=8,'mp'=4] {'dp'}, use_global_device_ids=true, to_apply=%region_6.7 | all-reduce | flops 6144 | bytes 49152 | tf_op jit(solution)/shard_map/psum | solution.py:76
  2013.0 4.4 multiply_reduce_fusion.1
  2017.4 2.2 multiply_reduce_fusion
  2019.7 37.1 %all-reduce = (f32[]{:T(128)}, f32[]{:T(128)}) all-reduce(f32[]{:T(128)} %multiply_reduce_fusion.1, f32[]{:T(128)} %multiply_reduce_fusion), channel_id=1, replica_groups=mesh['dp'=8,'mp'=4] {'dp','mp'}, use_global_device_ids=true, to_apply=%region_8.9 | all-reduce | flops 2 | bytes 16 | tf_op jit(solution)/shard_map/psum | solution.py:83
  2058.2 5.6 fusion.4
  2063.7 5.7 fusion.5
  (45 shorter events, 0.3 us)
Async XLA Ops:
  7.2 9.1 copy-start
  7.2 369.6 %all-gather.3.cloned.1.call-start = ((), (), s32[]{:S(2)}) async-start(), calls=%async_computation.2 | async-start | bytes 21233664 | tf_op jit(solution)/shard_map/all_gather | solution.py:60
  11.5 729.8 %all-gather.5.cloned.1.call-start = ((), (), s32[]{:S(2)}) async-start(), calls=%async_computation.3 | async-start | bytes 21233664 | tf_op jit(solution)/shard_map/all_gather | solution.py:54
  15.6 0.7 copy-start.15
  15.6 1348.4 %reduce-scatter.3.cloned.1.call-start = ((), (), s32[]{:S(2)}) async-start(), calls=%async_computation.4 | async-start | bytes 42467328 | tf_op jit(solution)/shard_map/reduce_scatter | solution.py:66
  18.2 358.5 %copy-start.5 = (bf16[128,3072]{1,0:T(8,128)(2,1)S(1)}, bf16[128,3072]{1,0:T(8,128)(2,1)}, u32[]{:S(2)}) copy-start(bf16[128,3072]{1,0:T(8,128)(2,1)} %param.12) | copy-start | bytes 2359300
  21.4 719.9 %copy-start.3 = (bf16[128,3072]{1,0:T(8,128)(2,1)S(1)}, bf16[128,3072]{1,0:T(8,128)(2,1)}, u32[]{:S(2)}) copy-start(bf16[128,3072]{1,0:T(8,128)(2,1)} %gather_fusion) | copy-start | bytes 2359300
  21.4 719.9 %copy-start.6 = (f32[3072]{0:T(1024)S(1)}, f32[3072]{0:T(1024)}, u32[]{:S(2)}) copy-start(f32[3072]{0:T(1024)} %param.13) | copy-start | bytes 36868
  741.3 8.0 copy-start.4
  764.3 1203.4 %reduce-scatter.5.cloned.1.call-start = ((), (), s32[]{:S(2)}) async-start(), calls=%async_computation.5 | async-start | bytes 42467328 | tf_op jit(solution)/shard_map/reduce_scatter | solution.py:63
  1367.2 645.7 %copy-start.13 = (f32[384]{0:T(512)S(1)}, f32[384]{0:T(512)}, u32[]{:S(2)}) copy-start(f32[384]{0:T(512)} %param.18) | copy-start | bytes 4612
  1367.2 645.7 %copy-start.14 = (f32[384]{0:T(512)S(1)}, f32[384]{0:T(512)}, u32[]{:S(2)}) copy-start(f32[384]{0:T(512)} %param.16) | copy-start | bytes 4612
  1367.2 645.7 %copy-start.11 = (f32[3072]{0:T(1024)S(1)}, f32[3072]{0:T(1024)}, u32[]{:S(2)}) copy-start(f32[3072]{0:T(1024)} %param.19) | copy-start | bytes 36868
  1367.3 645.7 %copy-start.12 = (f32[3072]{0:T(1024)S(1)}, f32[3072]{0:T(1024)}, u32[]{:S(2)}) copy-start(f32[3072]{0:T(1024)} %param.17) | copy-start | bytes 36868
  2012.9 45.2 %copy-start.10 = (f32[384]{0:T(512)}, f32[384]{0:T(512)S(1)}, u32[]{:S(2)}) copy-start(f32[384]{0:T(512)S(1)} %get-tuple-element.19) | copy-start | bytes 4612
  2012.9 50.8 %copy-start.9 = (f32[384]{0:T(512)}, f32[384]{0:T(512)S(1)}, u32[]{:S(2)}) copy-start(f32[384]{0:T(512)S(1)} %get-tuple-element.18) | copy-start | bytes 4612
  2013.0 45.2 %copy-start.8 = (f32[3072]{0:T(1024)}, f32[3072]{0:T(1024)S(1)}, u32[]{:S(2)}) copy-start(f32[3072]{0:T(1024)S(1)} %get-tuple-element.17) | copy-start | bytes 36868
  2013.0 50.7 %copy-start.7 = (f32[3072]{0:T(1024)}, f32[3072]{0:T(1024)S(1)}, u32[]{:S(2)}) copy-start(f32[3072]{0:T(1024)S(1)} %get-tuple-element.16) | copy-start | bytes 36868
  2013.0 4.4 copy-start.2
  2063.7 5.7 copy-start.1
Sparse Core Ops, SparseCore 0:
  11.6 365.1 all-gather.2
  378.9 362.3 all-gather.4
  764.4 599.5 reduce-scatter.2
  1367.8 599.8 reduce-scatter.4
where the time goes:
time: 2080 us
  waiting for transfers between devices  1890 us (91%)
  blocking collectives  79.1 us (4%)
  matrix products  48.6 us (2%)
  other arithmetic  35.7 us (2%)
    reduce_scatter x1, waiting for transfers between devices, on_device(): lax.psum_scatter(contract_tokens(out_grad, hidden_act), 'dp', scatter_dim...  600 us
    reduce_scatter x1, waiting for transfers between devices, on_device(): lax.psum_scatter(contract_tokens(normed, pre_grad), 'dp', scatter_dimensi...  584 us
    all_gather x1, waiting for transfers between devices, on_device(): lax.all_gather(w_down, 'dp', axis=0, tiled=True)  355 us
    all_gather x1, waiting for transfers between devices, on_device(): lax.all_gather(w_up, 'dp', axis=0, tiled=True)  354 us
  transfers between devices with their start and end apart: 4, of which 4 were waited for; matrix products, arithmetic and copies ran while one was open for 2% of the time, Pallas kernels for 0%

commit v1 on v0

--- a/solution.py
+++ b/solution.py
@@ -1,6 +1,9 @@
+import functools
 import jax
 import jax.numpy as jnp
 from jax import lax
+from jax.experimental import pallas as pl
+from jax.experimental.pallas import tpu as pltpu
 from jax.sharding import PartitionSpec as P
 
 decay_rate = 0.8
@@ -27,6 +30,286 @@
 
 def finish_update(grad, row_new, col_new):
     return grad * lax.rsqrt(row_new[:, None] * col_new[None, :])
+
+
+def gathered_grads(normed, out_grad, w_up, w_down):
+    left = normed
+    pre_act = jnp.dot(
+        left, lax.all_gather(w_up, "dp", axis=0, tiled=True), preferred_element_type=jnp.float32
+    )
+    act_value, pull_back = jax.vjp(gelu_tanh, pre_act)
+    hidden_act = act_value.astype(jnp.bfloat16)
+    left = out_grad
+    act_grad = jnp.dot(
+        left, lax.all_gather(w_down, "dp", axis=0, tiled=True), preferred_element_type=jnp.float32
+    )
+    pre_grad = pull_back(act_grad)[0].astype(jnp.bfloat16)
+    grad_down = lax.psum_scatter(
+        contract_tokens(out_grad, hidden_act), "dp", scatter_dimension=0, tiled=True
+    )
+    grad_up = lax.psum_scatter(
+        contract_tokens(normed, pre_grad), "dp", scatter_dimension=0, tiled=True
+    )
+    return grad_up, grad_down
+
+
+MESH = pl.DeviceIdType.MESH
+
+
+def flipped(index):
+    return index + 1 - 2 * lax.rem(index, 2)
+
+
+def greet(devices):
+    barrier = pltpu.get_barrier_semaphore()
+    for device in devices:
+        pl.semaphore_signal(barrier, inc=1, device_id=device, device_id_type=MESH)
+    pl.semaphore_wait(barrier, len(devices))
+
+
+def send(src, dst, send_sem, recv_sem, device):
+    return pltpu.make_async_remote_copy(
+        src_ref=src,
+        dst_ref=dst,
+        send_sem=send_sem,
+        recv_sem=recv_sem,
+        device_id=device,
+        device_id_type=MESH,
+    )
+
+
+def spread_kernel(
+    n,
+    act_a,
+    act_b,
+    mat_a,
+    mat_b,
+    all_a,
+    all_b,
+    cut_a,
+    cut_b,
+    own_act,
+    own_mat,
+    local_sem,
+    act_send,
+    act_recv,
+    mat_send,
+    mat_recv,
+):
+    me = lax.axis_index("dp")
+    col = lax.axis_index("mp")
+    tokens = act_a.shape[0]
+    part = tokens // 4
+    rows = mat_a.shape[0]
+    width = mat_a.shape[1] // n
+    beside = flipped(me)
+    core = flipped(col)
+    across = lax.rem(col + 2, 4)
+    acts = ((act_a, all_a), (act_b, all_b))
+    mats = ((mat_a, cut_a), (mat_b, cut_b))
+    others = [lax.rem(me + shift, n) for shift in range(1, n)]
+    greet([(other, col) for other in others] + [(me, core), (me, across)])
+
+    def rows_of(owner, quarter):
+        return pl.ds(pl.multiple_of(owner * tokens + quarter * part, part), part)
+
+    loads, stores = [], []
+    for k in range(2):
+        loads.append(pltpu.make_async_copy(acts[k][0], own_act.at[k], local_sem.at[k]))
+        stores.append(
+            pltpu.make_async_copy(
+                own_act.at[k],
+                acts[k][1].at[pl.ds(pl.multiple_of(me * tokens, tokens), tokens)],
+                local_sem.at[k],
+            )
+        )
+        cols = pl.ds(pl.multiple_of(me * width, width), width)
+        loads.append(pltpu.make_async_copy(mats[k][0].at[:, cols], own_mat.at[k], local_sem.at[2 + k]))
+        stores.append(
+            pltpu.make_async_copy(
+                own_mat.at[k],
+                mats[k][1].at[pl.ds(pl.multiple_of(me * rows, rows), rows)],
+                local_sem.at[2 + k],
+            )
+        )
+
+    sent = []
+    slots = [0]
+
+    def post(k, src, owner, quarter, device):
+        slot = slots[0]
+        slots[0] += 1
+        copy = send(
+            src, acts[k][1].at[rows_of(owner, quarter)], act_send.at[slot], act_recv.at[slot], device
+        )
+        copy.start()
+        sent.append(copy)
+        return copy
+
+    def own_rows(k):
+        return acts[k][0].at[pl.ds(pl.multiple_of(col * part, part), part)]
+
+    far = [lax.rem(me + 2 * shift, n) for shift in range(1, n // 2)]
+    from_far = [lax.rem(me + n - 2 * shift, n) for shift in range(1, n // 2)]
+    along = [[post(k, own_rows(k), me, col, (other, col)) for other in far] for k in range(2)]
+    over = [[post(k, own_rows(k), me, col, (beside, col))] for k in range(2)]
+    mat_sent = []
+    for k in range(2):
+        for shift in range(1, n):
+            other = others[shift - 1]
+            copy = send(
+                mats[k][0].at[:, pl.ds(pl.multiple_of(other * width, width), width)],
+                mats[k][1].at[pl.ds(pl.multiple_of(me * rows, rows), rows)],
+                mat_send.at[k, shift - 1],
+                mat_recv.at[k, shift - 1],
+                (other, col),
+            )
+            copy.start()
+            mat_sent.append(copy)
+    for load in loads:
+        load.start()
+    for load, store in zip(loads, stores):
+        load.wait()
+        store.start()
+
+    def held(k, owner, quarter):
+        return acts[k][1].at[rows_of(owner, quarter)]
+
+    crossed = [[], []]
+    shared = [[], []]
+    for k in range(2):
+        for slot, owner in enumerate(from_far):
+            along[k][slot].wait_recv()
+            over[k].append(post(k, held(k, owner, col), owner, col, (beside, col)))
+            crossed[k].append((owner, post(k, held(k, owner, col), owner, col, (me, across))))
+            shared[k].append(post(k, held(k, owner, col), owner, col, (me, core)))
+    for k in range(2):
+        for copy, owner in zip(over[k], [beside] + [flipped(owner) for owner in from_far]):
+            copy.wait_recv()
+            crossed[k].append((owner, post(k, held(k, owner, col), owner, col, (me, across))))
+            shared[k].append(post(k, held(k, owner, col), owner, col, (me, core)))
+    for k in range(2):
+        for owner, copy in crossed[k]:
+            copy.wait_recv()
+            shared[k].append(post(k, held(k, owner, across), owner, across, (me, core)))
+    for k in range(2):
+        for copy in shared[k]:
+            copy.wait_recv()
+    for copy in mat_sent:
+        copy.wait_recv()
+    for copy in sent + mat_sent:
+        copy.wait_send()
+    for store in stores:
+        store.wait()
+
+
+def spread(act_a, act_b, mat_a, mat_b):
+    n = lax.axis_size("dp")
+    tokens, depth = act_a.shape
+    rows, width = mat_a.shape[0], mat_a.shape[1] // n
+    slots = 2 * ((n // 2 - 1) + 1 + (n // 2 - 1) + (n - 1) + 2 * (n - 1))
+    anywhere = pl.BlockSpec(memory_space=pl.ANY)
+    return pl.pallas_call(
+        functools.partial(spread_kernel, n),
+        out_shape=(
+            jax.ShapeDtypeStruct((tokens * n, depth), act_a.dtype),
+            jax.ShapeDtypeStruct((tokens * n, depth), act_a.dtype),
+            jax.ShapeDtypeStruct((rows * n, width), mat_a.dtype),
+            jax.ShapeDtypeStruct((rows * n, width), mat_a.dtype),
+        ),
+        in_specs=[anywhere] * 4,
+        out_specs=(anywhere,) * 4,
+        scratch_shapes=[
+            pltpu.VMEM((2, tokens, depth), act_a.dtype),
+            pltpu.VMEM((2, rows, width), mat_a.dtype),
+            pltpu.SemaphoreType.DMA((4,)),
+            pltpu.SemaphoreType.DMA((slots,)),
+            pltpu.SemaphoreType.DMA((slots,)),
+            pltpu.SemaphoreType.DMA((2, n - 1)),
+            pltpu.SemaphoreType.DMA((2, n - 1)),
+        ],
+        compiler_params=pltpu.CompilerParams(collective_id=0, has_side_effects=True),
+    )(act_a, act_b, mat_a, mat_b)
+
+
+def return_kernel(n, mat_a, mat_b, out_a, out_b, own_mat, local_sem, mat_send, mat_recv):
+    me = lax.axis_index("dp")
+    col = lax.axis_index("mp")
+    rows, width = mat_a.shape[0] // n, mat_a.shape[1]
+    others = [lax.rem(me + shift, n) for shift in range(1, n)]
+    greet([(other, col) for other in others])
+    mats = ((mat_a, out_a), (mat_b, out_b))
+    cols = pl.ds(pl.multiple_of(me * width, width), width)
+    sent = []
+    for k in range(2):
+        for shift in range(1, n):
+            other = others[shift - 1]
+            copy = send(
+                mats[k][0].at[pl.ds(pl.multiple_of(other * rows, rows), rows)],
+                mats[k][1].at[:, cols],
+                mat_send.at[k, shift - 1],
+                mat_recv.at[k, shift - 1],
+                (other, col),
+            )
+            copy.start()
+            sent.append(copy)
+    loads, stores = [], []
+    for k in range(2):
+        mine = mats[k][0].at[pl.ds(pl.multiple_of(me * rows, rows), rows)]
+        loads.append(pltpu.make_async_copy(mine, own_mat.at[k], local_sem.at[k]))
+        stores.append(pltpu.make_async_copy(own_mat.at[k], mats[k][1].at[:, cols], local_sem.at[k]))
+        loads[k].start()
+    for load, store in zip(loads, stores):
+        load.wait()
+        store.start()
+    for copy in sent:
+        copy.wait()
+    for store in stores:
+        store.wait()
+
+
+def returned(mat_a, mat_b):
+    n = lax.axis_size("dp")
+    rows, width = mat_a.shape[0] // n, mat_a.shape[1]
+    anywhere = pl.BlockSpec(memory_space=pl.ANY)
+    return pl.pallas_call(
+        functools.partial(return_kernel, n),
+        out_shape=(jax.ShapeDtypeStruct((rows, width * n), mat_a.dtype),) * 2,
+        in_specs=[anywhere] * 2,
+        out_specs=(anywhere,) * 2,
+        scratch_shapes=[
+            pltpu.VMEM((2, rows, width), mat_a.dtype),
+            pltpu.SemaphoreType.DMA((2,)),
+            pltpu.SemaphoreType.DMA((2, n - 1)),
+            pltpu.SemaphoreType.DMA((2, n - 1)),
+        ],
+        compiler_params=pltpu.CompilerParams(collective_id=1, has_side_effects=True),
+    )(mat_a, mat_b)
+
+
+def suits_exchange(master, normed):
+    n = lax.axis_size("dp")
+    return (
+        lax.axis_size("mp") == 4
+        and 4 <= n <= 8
+        and n % 2 == 0
+        and master.shape[1] % (n * 128) == 0
+        and master.shape[0] % 16 == 0
+        and normed.shape[0] % 64 == 0
+    )
+
+
+def exchanged_grads(normed, out_grad, w_up, w_down):
+    normed_all, out_grad_all, cut_up, cut_down = spread(normed, out_grad, w_up, w_down)
+    pre_act = jnp.dot(normed_all, cut_up, preferred_element_type=jnp.float32)
+    act_value, pull_back = jax.vjp(gelu_tanh, pre_act)
+    hidden_act = act_value.astype(jnp.bfloat16)
+    act_grad = jnp.dot(out_grad_all, cut_down, preferred_element_type=jnp.float32)
+    pre_grad = pull_back(act_grad)[0].astype(jnp.bfloat16)
+    grad_up = contract_tokens(normed_all, pre_grad).astype(jnp.bfloat16)
+    grad_down = contract_tokens(out_grad_all, hidden_act).astype(jnp.bfloat16)
+    grad_up, grad_down = returned(grad_up, grad_down)
+    return grad_up.astype(jnp.float32), grad_down.astype(jnp.float32)
 
 
 def on_device(
@@ -49,23 +332,10 @@
     breadth = grid_cols * lax.axis_size("mp")
     w_up = master_up.astype(jnp.bfloat16)
     w_down = master_down.astype(jnp.bfloat16)
-    left = normed
-    pre_act = jnp.dot(
-        left, lax.all_gather(w_up, "dp", axis=0, tiled=True), preferred_element_type=jnp.float32
-    )
-    act_value, pull_back = jax.vjp(gelu_tanh, pre_act)
-    hidden_act = act_value.astype(jnp.bfloat16)
-    left = out_grad
-    act_grad = jnp.dot(
-        left, lax.all_gather(w_down, "dp", axis=0, tiled=True), preferred_element_type=jnp.float32
-    )
-    pre_grad = pull_back(act_grad)[0].astype(jnp.bfloat16)
-    grad_down = lax.psum_scatter(
-        contract_tokens(out_grad, hidden_act), "dp", scatter_dimension=0, tiled=True
-    )
-    grad_up = lax.psum_scatter(
-        contract_tokens(normed, pre_grad), "dp", scatter_dimension=0, tiled=True
-    )
+    if suits_exchange(master_up, normed):
+        grad_up, grad_down = exchanged_grads(normed, out_grad, w_up, w_down)
+    else:
+        grad_up, grad_down = gathered_grads(normed, out_grad, w_up, w_down)
     squares_up = grad_up * grad_up + tiny_value
     squares_down = grad_down * grad_down + tiny_value
     rowpart_up = jnp.sum(squares_up, axis=1)

time: 2080 us -> 387 us (0.19)
  waiting for transfers between devices: 1890 us -> 0 us
  Pallas kernels: 0 us -> 231 us
  matrix products: 48.6 us -> 20.1 us
    reduce_scatter x2 -> x0, waiting for transfers between devices: 1180 us -> none  [the longest x1 600 us: on_device(): lax.psum_scatter(contract_tokens(out_grad, hidden_act), 'dp', scatter_dim...]
    all_gather x2 -> x0, waiting for transfers between devices: 710 us -> none  [the longest x1 355 us: on_device(): lax.all_gather(w_down, 'dp', axis=0, tiled=True)]
    pallas_call x0 -> x2, Pallas kernels: none -> 231 us  [the longest x1 126 us: spread(): pl.pallas_call(functools.partial(spread_kernel, n), out_shape=(jax.ShapeD...]
  transfers between devices with their start and end apart: 4 -> 0, of which waited for: 4 -> 0; matrix products, arithmetic and copies ran while one was open for 2% -> 0% of each run, Pallas kernels for 0% -> 0%
where the time goes in v1:
time: 387 us; the launch traced here: 386 us
  Pallas kernels  231 us (60%)
  blocking collectives  96.6 us (25%)
  other arithmetic  33.2 us (9%)
  matrix products  20.1 us (5%)
    pallas_call x1, Pallas kernels, spread(): pl.pallas_call(functools.partial(spread_kernel, n), out_shape=(jax.ShapeD...  126 us
    pallas_call x1, Pallas kernels, returned(): pl.pallas_call(functools.partial(return_kernel, n), out_shape=(jax.ShapeD...  105 us
    psum x1, blocking collectives, on_device(): colsum_up, colsum_down = lax.psum((colpart_up, colpart_down), 'dp')  53.8 us
    psum x1, blocking collectives, on_device(): lax.psum((jnp.sum(raw_up * raw_up), jnp.sum(raw_down * raw_down)), ('dp',...  37.1 us
    dot_general x2, matrix products, contract_tokens(): lax.dot_general(left, right, (((0,), (0,)), ((), ())), preferred_element_...  10.1 us

profile of v1, /device:TPU:0, one launch (start us, length us, event | category | flops | bytes accessed | tf_op | source)
XLA Modules:
  0.0 385.6 jit_solution(1924025189543656783)
XLA Ops:
  0.6 0.0 copy-start
  0.6 0.8 compare_and_fusion
  1.5 0.8 compare_select_fusion
  2.3 0.3 copy-done
  2.5 1.9 gather_fusion
  4.5 1.4 convert_reduce_fusion
  5.9 1.5 fusion.10
  7.5 2.4 fusion.12.act_a
  9.9 4.2 %convert_element_type.32.mat_a = bf16[384,3072]{1,0:T(8,128)(2,1)} convert(f32[384,3072]{1,0:T(8,128)} %param.14) | non-fusion elementwise | flops 1179648 | bytes 7077888 | tf_op jit(solution)/shard_map/convert_element_type | solution.py:333
  14.1 1.7 convert_element_type.33.mat_b
  15.9 125.8 %shard_map.145 = (bf16[1024,3072]{1,0:T(8,128)(2,1)}, bf16[1024,3072]{1,0:T(8,128)(2,1)}, bf16[3072,384]{1,0:T(8,128)(2,1)}, bf16[3072,384]{1,0:T(8,128)(2,1)}) custom-call(bf16[128,3072]{1,0:T(8,128)(2,1)} %fusion.12.act_a, bf16[128,3072]{1,0:T(8,128)(2,1)} %act_b.1, bf16[384,3072]{1,0:T(8,128)(2,1)} %convert_element_type.32.mat_a, ...), custom_call_target="tpu_custom_call" | custom-call | tf_op jit(solution)/shard_map/pallas_call | solution.py:212
  141.7 6.5 %fusion.41 = f32[1024,384]{1,0:T(8,128)S(1)} fusion(bf16[1024,3072]{1,0:T(8,128)(2,1)} %get-tuple-element.13, bf16[3072,384]{1,0:T(8,128)(2,1)} %get-tuple-element.14), kind=kOutput, calls=%fused_computation.64 | convolution fusion | flops 2415919104 | bytes 10223616 | tf_op jit(solution)/shard_map/dot_general | solution.py:307
  148.3 3.4 fusion.42
  151.7 5.2 %convolution_convert_fusion.1.mat_a = bf16[3072,384]{1,0:T(8,128)(2,1)} fusion(bf16[1024,3072]{1,0:T(8,128)(2,1)S(1)} %copy-done.13, f32[1024,384]{1,0:T(8,128)S(1)} %fusion.42, f32[1024,384]{1,0:T(8,128)S(1)} %fusion.41), kind=kOutput, calls=%fused_computation.16 | convolution fusion | flops 2424963072 | bytes 11796480 | tf_op jit(solution)/shard_map/dot_general | solution.py:26
  156.9 4.9 %convolution_convert_fusion.mat_b = bf16[3072,384]{1,0:T(8,128)(2,1)} fusion(bf16[1024,3072]{1,0:T(8,128)(2,1)S(1)} %bitcast.7, f32[1024,384]{1,0:T(8,128)S(1)} %fusion.42), kind=kOutput, calls=%fused_computation.15 | convolution fusion | flops 2420637696 | bytes 10223616 | tf_op jit(solution)/shard_map/dot_general | solution.py:26
  161.8 105.3 %shard_map.146 = (bf16[384,3072]{1,0:T(8,128)(2,1)}, bf16[384,3072]{1,0:T(8,128)(2,1)}) custom-call(bf16[3072,384]{1,0:T(8,128)(2,1)} %convolution_convert_fusion.1.mat_a, bf16[3072,384]{1,0:T(8,128)(2,1)} %convolution_convert_fusion.mat_b), custom_call_target="tpu_custom_call" | custom-call | tf_op jit(solution)/shard_map/pallas_call | solution.py:275
  267.2 6.3 %fusion.2 = (f32[384]{0:T(512)S(1)}, f32[3072]{0:T(1024)S(1)}, f32[3072]{0:T(1024)S(1)}, f32[384]{0:T(512)S(1)}) fusion(bf16[384,3072]{1,0:T(8,128)(2,1)} %get-tuple-element.16, bf16[384,3072]{1,0:T(8,128)(2,1)} %get-tuple-element.17), kind=kLoop, calls=%fused_computation.7 | loop fusion | flops 11789568 | bytes 4746240 | tf_op jit(solution)/shard_map/reduce_sum | solution.py:341
  273.5 5.7 %all-reduce.2 = (f32[384]{0:T(512)S(1)}, f32[384]{0:T(512)S(1)}) all-reduce(f32[384]{0:T(512)S(1)} %get-tuple-element.20, f32[384]{0:T(512)S(1)} %get-tuple-element.29), channel_id=1, replica_groups=mesh['dp'=8,'mp'=4] {'mp'}, use_global_device_ids=true, to_apply=%region_3.4 | all-reduce | flops 768 | bytes 6144 | tf_op jit(solution)/shard_map/psum | solution.py:345
  279.3 53.8 %all-reduce.1 = (f32[3072]{0:T(1024)S(1)}, f32[3072]{0:T(1024)S(1)}) all-reduce(f32[3072]{0:T(1024)S(1)} %get-tuple-element.21, f32[3072]{0:T(1024)S(1)} %get-tuple-element.28), channel_id=1, replica_groups=mesh['dp'=8,'mp'=4] {'dp'}, use_global_device_ids=true, to_apply=%region_5.6 | all-reduce | flops 6144 | bytes 49152 | tf_op jit(solution)/shard_map/psum | solution.py:346
  333.1 3.8 multiply_reduce_fusion.1
  336.9 2.1 multiply_reduce_fusion
  339.0 37.1 %all-reduce = (f32[]{:T(128)}, f32[]{:T(128)}) all-reduce(f32[]{:T(128)} %multiply_reduce_fusion.1, f32[]{:T(128)} %multiply_reduce_fusion), channel_id=1, replica_groups=mesh['dp'=8,'mp'=4] {'dp','mp'}, use_global_device_ids=true, to_apply=%region_7.8 | all-reduce | flops 2 | bytes 16 | tf_op jit(solution)/shard_map/psum | solution.py:353
  377.6 4.9 %fusion.7 = f32[384,3072]{1,0:T(8,128)} fusion(bf16[384,3072]{1,0:T(8,128)(2,1)} %get-tuple-element.16, f32[]{:T(128)S(6)} %max.6, f32[3072]{0:T(1024)S(1)} %multiply_add_fusion.1, f32[384]{0:T(512)S(1)} %multiply_add_fusion.3), kind=kLoop, calls=%fused_computation.14 | loop fusion | flops 4718592 | bytes 7091716 | tf_op jit(solution)/shard_map/div | solution.py:356
  382.5 3.1 fusion.6
  (40 shorter events, 0.1 us)
Async XLA Ops:
  0.6 1.9 copy-start
  2.5 4.9 %copy-start.8 = (f32[3072]{0:T(1024)S(1)}, f32[3072]{0:T(1024)}, u32[]{:S(2)}) copy-start(f32[3072]{0:T(1024)} %param.13) | copy-start | bytes 36868
  9.9 4.2 %copy-start.3 = (f32[384,3072]{1,0:T(8,128)S(1)}, f32[384,3072]{1,0:T(8,128)}, u32[]{:S(2)}) copy-start(f32[384,3072]{1,0:T(8,128)} %param.15) | copy-start | bytes 14155780
  141.7 6.6 %copy-start.13 = (bf16[1024,3072]{1,0:T(8,128)(2,1)S(1)}, bf16[1024,3072]{1,0:T(8,128)(2,1)}, u32[]{:S(2)}) copy-start(bf16[1024,3072]{1,0:T(8,128)(2,1)} %get-tuple-element.12) | copy-start | bytes 18874372
  141.7 6.6 %copy-start.14 = (bf16[3072,384]{1,0:T(8,128)(2,1)S(1)}, bf16[3072,384]{1,0:T(8,128)(2,1)}, u32[]{:S(2)}) copy-start(bf16[3072,384]{1,0:T(8,128)(2,1)} %get-tuple-element.15) | copy-start | bytes 7077892
  148.3 8.7 %slice-start = ((s8[6291456]{0:T(1024)(128)(4,1)}), s8[4194304]{0:T(1024)(128)(4,1)S(1)}, s32[]{:S(2)}) async-start(s8[6291456]{0:T(1024)(128)(4,1)} %bitcast.6), calls=%async_computation | async-start | bytes 8388608
  151.7 5.2 %slice-start.1 = ((s8[6291456]{0:T(1024)(128)(4,1)}), s8[2097152]{0:T(1024)(128)(4,1)S(1)}, s32[]{:S(2)}) async-start(s8[6291456]{0:T(1024)(128)(4,1)} %bitcast.6), calls=%async_computation.1 | async-start | bytes 4194304
  267.2 12.0 %copy-start.11 = (f32[384]{0:T(512)S(1)}, f32[384]{0:T(512)}, u32[]{:S(2)}) copy-start(f32[384]{0:T(512)} %param.16) | copy-start | bytes 4612
  267.2 12.0 %copy-start.12 = (f32[384]{0:T(512)S(1)}, f32[384]{0:T(512)}, u32[]{:S(2)}) copy-start(f32[384]{0:T(512)} %param.18) | copy-start | bytes 4612
  267.2 65.9 %copy-start.9 = (f32[3072]{0:T(1024)S(1)}, f32[3072]{0:T(1024)}, u32[]{:S(2)}) copy-start(f32[3072]{0:T(1024)} %param.17) | copy-start | bytes 36868
  273.5 63.4 %copy-start.10 = (f32[3072]{0:T(1024)S(1)}, f32[3072]{0:T(1024)}, u32[]{:S(2)}) copy-start(f32[3072]{0:T(1024)} %param.19) | copy-start | bytes 36868
  279.2 98.3 %copy-start.6 = (f32[384]{0:T(512)}, f32[384]{0:T(512)S(1)}, u32[]{:S(2)}) copy-start(f32[384]{0:T(512)S(1)} %multiply_add_fusion.3) | copy-start | bytes 4612
  279.2 103.2 %copy-start.7 = (f32[384]{0:T(512)}, f32[384]{0:T(512)S(1)}, u32[]{:S(2)}) copy-start(f32[384]{0:T(512)S(1)} %multiply_add_fusion.2) | copy-start | bytes 4612
  333.1 3.8 copy-start.1
  333.1 44.4 %copy-start.4 = (f32[3072]{0:T(1024)}, f32[3072]{0:T(1024)S(1)}, u32[]{:S(2)}) copy-start(f32[3072]{0:T(1024)S(1)} %multiply_add_fusion.1) | copy-start | bytes 36868
  336.9 45.6 %copy-start.5 = (f32[3072]{0:T(1024)}, f32[3072]{0:T(1024)S(1)}, u32[]{:S(2)}) copy-start(f32[3072]{0:T(1024)S(1)} %multiply_add_fusion) | copy-start | bytes 36868
  377.6 4.9 %copy-start.2 = (bf16[384,3072]{1,0:T(8,128)(2,1)S(1)}, bf16[384,3072]{1,0:T(8,128)(2,1)}, u32[]{:S(2)}) copy-start(bf16[384,3072]{1,0:T(8,128)(2,1)} %get-tuple-element.17) | copy-start | bytes 7077892

commit v2 on v1

--- a/solution.py
+++ b/solution.py
@@ -232,15 +232,49 @@
     )(act_a, act_b, mat_a, mat_b)
 
 
-def return_kernel(n, mat_a, mat_b, out_a, out_b, own_mat, local_sem, mat_send, mat_recv):
+def return_kernel(
+    n,
+    breadth,
+    mat_a,
+    mat_b,
+    stats,
+    row_old,
+    out_a,
+    out_b,
+    gathered,
+    row_new,
+    energy,
+    own_mat,
+    stat_buf,
+    line_buf,
+    energy_buf,
+    local_sem,
+    mat_send,
+    mat_recv,
+    stat_send,
+    stat_recv,
+    line_send,
+    line_recv,
+    energy_send,
+    energy_recv,
+):
     me = lax.axis_index("dp")
     col = lax.axis_index("mp")
     rows, width = mat_a.shape[0] // n, mat_a.shape[1]
     others = [lax.rem(me + shift, n) for shift in range(1, n)]
-    greet([(other, col) for other in others])
+    sources = [lax.rem(me + n - shift, n) for shift in range(1, n)]
+    siblings = [lax.rem(col + shift, 4) for shift in range(1, 4)]
+    greet([(other, col) for other in others] + [(me, other) for other in siblings])
     mats = ((mat_a, out_a), (mat_b, out_b))
     cols = pl.ds(pl.multiple_of(me * width, width), width)
-    sent = []
+    stat_sent = []
+    for shift, other in enumerate(others):
+        copy = send(
+            stats.at[other], stat_buf.at[me], stat_send.at[shift], stat_recv.at[shift], (other, col)
+        )
+        copy.start()
+        stat_sent.append(copy)
+    sent = [[], []]
     for k in range(2):
         for shift in range(1, n):
             other = others[shift - 1]
@@ -252,39 +286,97 @@
                 (other, col),
             )
             copy.start()
-            sent.append(copy)
+            sent[k].append(copy)
     loads, stores = [], []
     for k in range(2):
         mine = mats[k][0].at[pl.ds(pl.multiple_of(me * rows, rows), rows)]
         loads.append(pltpu.make_async_copy(mine, own_mat.at[k], local_sem.at[k]))
         stores.append(pltpu.make_async_copy(own_mat.at[k], mats[k][1].at[:, cols], local_sem.at[k]))
         loads[k].start()
+
+    for copy in stat_sent:
+        copy.wait_recv()
+    total = stats[me]
+    gathered[me] = total
+    for source in sources:
+        block = stat_buf[source]
+        gathered[source] = block
+        total = total + block
+    line_buf[col] = total
     for load, store in zip(loads, stores):
         load.wait()
         store.start()
-    for copy in sent:
-        copy.wait()
     for store in stores:
         store.wait()
-
-
-def returned(mat_a, mat_b):
+    line_sent = []
+    for shift, other in enumerate(siblings):
+        copy = send(
+            line_buf.at[col], line_buf.at[col], line_send.at[shift], line_recv.at[shift], (me, other)
+        )
+        copy.start()
+        line_sent.append(copy)
+    for copy in line_sent:
+        copy.wait_recv()
+    total = line_buf[0] + line_buf[1] + line_buf[2] + line_buf[3]
+    fresh = decay_rate * row_old[...] + (1.0 - decay_rate) * total[0:2] / breadth
+    row_new[0:2] = fresh
+    spent = jnp.sum(total[2:4] / fresh, axis=1, keepdims=True)
+    energy_buf[me] = jnp.broadcast_to(spent, (2, 128))
+    for copy in stat_sent + line_sent:
+        copy.wait_send()
+    sent[0][0].wait_recv()
+    energy_sent = []
+    for shift, other in enumerate(others):
+        copy = send(
+            energy_buf.at[me], energy_buf.at[me], energy_send.at[shift], energy_recv.at[shift], (other, col)
+        )
+        copy.start()
+        energy_sent.append(copy)
+    for copy in sent[0][1:] + sent[1] + energy_sent:
+        copy.wait_recv()
+    summed = energy_buf[0]
+    for source in range(1, n):
+        summed = summed + energy_buf[source]
+    energy[...] = summed
+    for copy in sent[0] + sent[1] + energy_sent:
+        copy.wait_send()
+
+
+def returned(mat_a, mat_b, stats, row_old, breadth):
     n = lax.axis_size("dp")
     rows, width = mat_a.shape[0] // n, mat_a.shape[1]
     anywhere = pl.BlockSpec(memory_space=pl.ANY)
+    vmem = pl.BlockSpec(memory_space=pltpu.VMEM)
+    peers = pltpu.SemaphoreType.DMA((n - 1,))
+    line = pltpu.SemaphoreType.DMA((3,))
     return pl.pallas_call(
-        functools.partial(return_kernel, n),
-        out_shape=(jax.ShapeDtypeStruct((rows, width * n), mat_a.dtype),) * 2,
-        in_specs=[anywhere] * 2,
-        out_specs=(anywhere,) * 2,
+        functools.partial(return_kernel, n, breadth),
+        out_shape=(
+            jax.ShapeDtypeStruct((rows, width * n), mat_a.dtype),
+            jax.ShapeDtypeStruct((rows, width * n), mat_a.dtype),
+            jax.ShapeDtypeStruct(stats.shape, jnp.float32),
+            jax.ShapeDtypeStruct(row_old.shape, jnp.float32),
+            jax.ShapeDtypeStruct((2, 128), jnp.float32),
+        ),
+        in_specs=[anywhere, anywhere, vmem, vmem],
+        out_specs=(anywhere, anywhere, vmem, vmem, vmem),
         scratch_shapes=[
             pltpu.VMEM((2, rows, width), mat_a.dtype),
+            pltpu.VMEM(stats.shape, jnp.float32),
+            pltpu.VMEM((4,) + stats.shape[1:], jnp.float32),
+            pltpu.VMEM((n, 2, 128), jnp.float32),
             pltpu.SemaphoreType.DMA((2,)),
             pltpu.SemaphoreType.DMA((2, n - 1)),
             pltpu.SemaphoreType.DMA((2, n - 1)),
+            peers,
+            peers,
+            line,
+            line,
+            peers,
+            peers,
         ],
         compiler_params=pltpu.CompilerParams(collective_id=1, has_side_effects=True),
-    )(mat_a, mat_b)
+    )(mat_a, mat_b, stats, row_old)
 
 
 def suits_exchange(master, normed):
@@ -295,21 +387,51 @@
         and n % 2 == 0
         and master.shape[1] % (n * 128) == 0
         and master.shape[0] % 16 == 0
+        and master.shape[0] * n == master.shape[1]
         and normed.shape[0] % 64 == 0
     )
 
 
-def exchanged_grads(normed, out_grad, w_up, w_down):
+def column_block(grad, col_old, depth):
+    width = grad.shape[1]
+    mine = lax.dynamic_slice_in_dim(col_old, lax.axis_index("dp") * width, width)
+    squares = grad * grad + tiny_value
+    col_new = decay_rate * mine + (1.0 - decay_rate) * jnp.sum(squares, axis=0) / depth
+    rowpart = jnp.sum(squares, axis=1)
+    spent = jnp.sum(grad * grad * (1.0 / col_new)[None, :], axis=1)
+    return rowpart, spent, col_new
+
+
+def exchanged_step(normed, out_grad, w_up, w_down, row_up, col_up, row_down, col_down):
+    n = lax.axis_size("dp")
+    rows, width = w_up.shape[0], w_up.shape[1] // n
+    depth = rows * n
+    breadth = width * n * lax.axis_size("mp")
     normed_all, out_grad_all, cut_up, cut_down = spread(normed, out_grad, w_up, w_down)
     pre_act = jnp.dot(normed_all, cut_up, preferred_element_type=jnp.float32)
     act_value, pull_back = jax.vjp(gelu_tanh, pre_act)
     hidden_act = act_value.astype(jnp.bfloat16)
     act_grad = jnp.dot(out_grad_all, cut_down, preferred_element_type=jnp.float32)
     pre_grad = pull_back(act_grad)[0].astype(jnp.bfloat16)
-    grad_up = contract_tokens(normed_all, pre_grad).astype(jnp.bfloat16)
-    grad_down = contract_tokens(out_grad_all, hidden_act).astype(jnp.bfloat16)
-    grad_up, grad_down = returned(grad_up, grad_down)
-    return grad_up.astype(jnp.float32), grad_down.astype(jnp.float32)
+    grad_down = contract_tokens(out_grad_all, hidden_act)
+    grad_up = contract_tokens(normed_all, pre_grad)
+    rowpart_up, spent_up, col_part_up = column_block(grad_up, col_up, depth)
+    rowpart_down, spent_down, col_part_down = column_block(grad_down, col_down, depth)
+    by_row = jnp.stack([rowpart_up, rowpart_down, spent_up, spent_down]).reshape(4, n, rows)
+    by_col = jnp.broadcast_to(jnp.stack([col_part_up, col_part_down])[:, None], (2, n, width))
+    stats = jnp.concatenate([by_row, by_col, jnp.zeros_like(by_col)]).transpose(1, 0, 2)
+    moved_up, moved_down, gathered, row_new, energy = returned(
+        grad_up.astype(jnp.bfloat16),
+        grad_down.astype(jnp.bfloat16),
+        stats,
+        jnp.stack([row_up, row_down]),
+        breadth,
+    )
+    col_new = gathered[:, 4:6].transpose(1, 0, 2).reshape(2, n * width)
+    shrink = jnp.maximum(1.0, jnp.sqrt(energy[:, 0] / (depth * breadth)))
+    update_up = finish_update(moved_up.astype(jnp.float32), row_new[0], col_new[0]) / shrink[0]
+    update_down = finish_update(moved_down.astype(jnp.float32), row_new[1], col_new[1]) / shrink[1]
+    return (update_up, update_down, row_new[0], col_new[0], row_new[1], col_new[1])
 
 
 def on_device(
@@ -333,9 +455,8 @@
     w_up = master_up.astype(jnp.bfloat16)
     w_down = master_down.astype(jnp.bfloat16)
     if suits_exchange(master_up, normed):
-        grad_up, grad_down = exchanged_grads(normed, out_grad, w_up, w_down)
-    else:
-        grad_up, grad_down = gathered_grads(normed, out_grad, w_up, w_down)
+        return exchanged_step(normed, out_grad, w_up, w_down, row_up, col_up, row_down, col_down)
+    grad_up, grad_down = gathered_grads(normed, out_grad, w_up, w_down)
     squares_up = grad_up * grad_up + tiny_value
     squares_down = grad_down * grad_down + tiny_value
     rowpart_up = jnp.sum(squares_up, axis=1)

time: 387 us -> 329 us (0.85)
  blocking collectives: 96.6 us -> 0 us
  Pallas kernels: 231 us -> 253 us
  local copies, waits for them, and re-layouts: 2.28 us -> 16.2 us
  matrix products: 20.1 us -> 30.6 us
  other arithmetic: 33.2 us -> 27.9 us
    psum x3 -> x0, blocking collectives: 96.6 us -> none  [the longest x1 53.8 us: on_device(): colsum_up, colsum_down = lax.psum((colpart_up, colpart_down), 'dp')]
    pallas_call x1, Pallas kernels: 105 us -> 127 us  [returned(): pl.pallas_call(functools.partial(return_kernel, n, breadth), out_shape=(j...]
    dot_general x2, matrix products: 10.1 us -> 22.4 us  [contract_tokens(): lax.dot_general(left, right, (((0,), (0,)), ((), ())), preferred_element_...]
    dot_general x0 -> x2, local copies, waits for them, and re-layouts: none -> 9.76 us  [contract_tokens(): lax.dot_general(left, right, (((0,), (0,)), ((), ())), preferred_element_...]
    reduce_sum x3 -> x2, other arithmetic: 12.2 us -> 4.2 us  [column_block(): spent = jnp.sum(grad * grad * (1.0 / col_new)[None, :], axis=1)]
    div x2 -> x3, other arithmetic: 8.01 us -> 10.1 us  [the longest x1 5.55 us: exchanged_step(): finish_update(moved_down.astype(jnp.float32), row_new[1], col_new[1])]
    dot_general x2 -> x1, matrix products: 9.96 us -> 8.22 us  [exchanged_step(): pre_act = jnp.dot(normed_all, cut_up, preferred_element_type=jnp.float32)]
where the time goes in v2:
time: 329 us; the launch traced here: 328 us
  Pallas kernels  253 us (77%)
  matrix products  30.6 us (9%)
  other arithmetic  27.9 us (8%)
  local copies, waits for them, and re-layouts  16.2 us (5%)
    pallas_call x1, Pallas kernels, returned(): pl.pallas_call(functools.partial(return_kernel, n, breadth), out_shape=(j...  127 us
    pallas_call x1, Pallas kernels, spread(): pl.pallas_call(functools.partial(spread_kernel, n), out_shape=(jax.ShapeD...  126 us
    dot_general x2, matrix products, contract_tokens(): lax.dot_general(left, right, (((0,), (0,)), ((), ())), preferred_element_...  22.4 us
    dot_general x2, local copies, waits for them, and re-layouts, contract_tokens(): lax.dot_general(left, right, (((0,), (0,)), ((), ())), preferred_element_...  9.76 us
    dot_general x1, matrix products, exchanged_step(): pre_act = jnp.dot(normed_all, cut_up, preferred_element_type=jnp.float32)  8.22 us

profile of v2, /device:TPU:0, one launch (start us, length us, event | category | flops | bytes accessed | tf_op | source)
XLA Modules:
  0.0 328.4 jit_solution(4684657380862363818)
XLA Ops:
  0.6 0.8 compare_select_fusion
  1.5 1.1 copy-done
  2.5 1.9 gather_fusion
  4.5 1.4 convert_reduce_fusion
  5.9 1.5 fusion.2
  7.5 2.4 fusion.4.act_a
  9.9 4.2 %convert_element_type.32.mat_a = bf16[384,3072]{1,0:T(8,128)(2,1)} convert(f32[384,3072]{1,0:T(8,128)} %param.14) | non-fusion elementwise | flops 1179648 | bytes 7077888 | tf_op jit(solution)/shard_map/convert_element_type | solution.py:455
  14.2 1.7 convert_element_type.33.mat_b
  15.9 125.8 %shard_map.145 = (bf16[1024,3072]{1,0:T(8,128)(2,1)}, bf16[1024,3072]{1,0:T(8,128)(2,1)}, bf16[3072,384]{1,0:T(8,128)(2,1)}, bf16[3072,384]{1,0:T(8,128)(2,1)}) custom-call(bf16[128,3072]{1,0:T(8,128)(2,1)} %fusion.4.act_a, bf16[128,3072]{1,0:T(8,128)(2,1)} %act_b.1, bf16[384,3072]{1,0:T(8,128)(2,1)} %convert_element_type.32.mat_a, ...), custom_call_target="tpu_custom_call" | custom-call | tf_op jit(solution)/shard_map/pallas_call | solution.py:212
  141.7 8.2 %fusion.38 = f32[1024,384]{1,0:T(8,128)} fusion(bf16[1024,3072]{1,0:T(8,128)(2,1)} %get-tuple-element.15, bf16[3072,384]{1,0:T(8,128)(2,1)} %get-tuple-element.18), kind=kOutput, calls=%fused_computation.67 | convolution fusion | flops 2415919104 | bytes 10223616 | tf_op jit(solution)/shard_map/dot_general | solution.py:411
  149.9 14.0 %add_reduce_fusion.2 = (f32[384]{0:T(512)S(1)}, f32[3072,384]{0,1:T(8,128)}) fusion(bf16[1024,3072]{1,0:T(8,128)(2,1)} %get-tuple-element.15, f32[1024,384]{1,0:T(8,128)} %fusion.38, bf16[1024,3072]{1,0:T(8,128)(2,1)} %get-tuple-element.16, bf16[3072,384]{1,0:T(8,128)(2,1)S(1)} %copy-done.12), kind=kOutput, calls=%fused_computation.7 | convolution fusion | flops 4843240960 | bytes 21235200 | tf_op jit(solution)/shard_map/dot_general | solution.py:26
  163.9 8.4 %add_reduce_fusion = (f32[384]{0:T(512)S(1)}, f32[3072,384]{0,1:T(8,128)}) fusion(bf16[1024,3072]{1,0:T(8,128)(2,1)} %get-tuple-element.16, f32[1024,384]{1,0:T(8,128)} %fusion.38), kind=kOutput, calls=%fused_computation.5 | convolution fusion | flops 2422996480 | bytes 12584448 | tf_op jit(solution)/shard_map/dot_general | solution.py:26
  172.3 0.8 broadcast_divide_fusion
  173.2 3.3 %multiply_reduce_fusion = (f32[3072]{0:T(1024)S(1)}, f32[3072]{0:T(1024)S(1)}) fusion(f32[3072,384]{0,1:T(8,128)} %get-tuple-element.41, f32[384]{0:T(512)S(1)} %get-tuple-element.30), kind=kLoop, calls=%fused_computation.3 | loop fusion | flops 5892096 | bytes 4744704 | tf_op jit(solution)/shard_map/reduce_sum | solution.py:401
  176.9 0.9 multiply_reduce_fusion.1
  177.9 0.7 concatenate.5
  178.6 4.9 %copy.16.mat_a = bf16[3072,384]{1,0:T(8,128)(2,1)} copy(f32[3072,384]{0,1:T(8,128)} %get-tuple-element.39) | data formatting | bytes 7077888 | tf_op jit(solution)/shard_map/dot_general | solution.py:26
  183.5 4.9 %copy.17.mat_b = bf16[3072,384]{1,0:T(8,128)(2,1)} copy(f32[3072,384]{0,1:T(8,128)} %get-tuple-element.41) | data formatting | bytes 7077888 | tf_op jit(solution)/shard_map/dot_general | solution.py:26
  189.0 127.1 %shard_map.146 = (bf16[384,3072]{1,0:T(8,128)(2,1)}, bf16[384,3072]{1,0:T(8,128)(2,1)}, f32[8,8,384]{2,1,0:T(8,128)}, f32[2,384]{1,0:T(2,128)}, f32[2,128]{1,0:T(2,128)}) custom-call(bf16[3072,384]{1,0:T(8,128)(2,1)} %copy.16.mat_a, bf16[3072,384]{1,0:T(8,128)(2,1)} %copy.17.mat_b, f32[8,8,384]{2,1,0:T(8,128)} %bitcast.25, f32[2,384]{1,0:T(2,128)} %pad_maximum_fusion.1.row_old), custom_call_target="tpu_custom_call" | custom-call | tf_op jit(solution)/shard_map/pallas_call | solution.py:352
  316.0 0.9 slice_bitcast_fusion
  317.0 0.8 slice_reduce_fusion
  317.8 0.7 sqrt_maximum_fusion
  319.0 5.6 %multiply_divide_fusion = f32[384,3072]{1,0:T(8,128)} fusion(bf16[384,3072]{1,0:T(8,128)(2,1)} %get-tuple-element.23, f32[]{:T(128)} %bitcast.9, f32[3072]{0:T(1024)S(1)} %bitcast.26, f32[384]{0:T(512)S(1)} %get-tuple-element.28), kind=kLoop, calls=%fused_computation.1 | loop fusion | flops 4718592 | bytes 7091716 | tf_op jit(solution)/shard_map/div | solution.py:433
  324.6 3.8 %multiply_divide_fusion.1 = f32[384,3072]{1,0:T(8,128)} fusion(bf16[384,3072]{1,0:T(8,128)(2,1)S(1)} %copy-done.4, f32[]{:T(128)} %bitcast.7, f32[3072]{0:T(1024)S(1)} %bitcast.28, f32[384]{0:T(512)S(1)} %get-tuple-element.29), kind=kLoop, calls=%fused_computation.2 | loop fusion | flops 4718592 | bytes 7091716 | tf_op jit(solution)/shard_map/div | solution.py:432
  (41 shorter events, 1.7 us)
Async XLA Ops:
  0.6 1.9 copy-start
  2.5 1.9 copy-start.13
  2.5 4.9 %copy-start.7 = (f32[3072]{0:T(1024)S(1)}, f32[3072]{0:T(1024)}, u32[]{:S(2)}) copy-start(f32[3072]{0:T(1024)} %param.13) | copy-start | bytes 36868
  9.9 4.2 %copy-start.3 = (f32[384,3072]{1,0:T(8,128)S(1)}, f32[384,3072]{1,0:T(8,128)}, u32[]{:S(2)}) copy-start(f32[384,3072]{1,0:T(8,128)} %param.15) | copy-start | bytes 14155780
  141.7 8.2 %copy-start.12 = (bf16[3072,384]{1,0:T(8,128)(2,1)S(1)}, bf16[3072,384]{1,0:T(8,128)(2,1)}, u32[]{:S(2)}) copy-start(bf16[3072,384]{1,0:T(8,128)(2,1)} %get-tuple-element.17) | copy-start | bytes 7077892
  173.2 3.8 %copy-start.2 = (f32[3072,384]{0,1:T(8,128)S(1)}, f32[3072,384]{0,1:T(8,128)}, u32[]{:S(2)}) copy-start(f32[3072,384]{0,1:T(8,128)} %get-tuple-element.39) | copy-start | bytes 14155780
  183.5 4.9 %copy-start.10 = (f32[384]{0:T(512)S(1)}, f32[384]{0:T(512)}, u32[]{:S(2)}) copy-start(f32[384]{0:T(512)} %param.16) | copy-start | bytes 4612
  183.5 4.9 %copy-start.11 = (f32[384]{0:T(512)S(1)}, f32[384]{0:T(512)}, u32[]{:S(2)}) copy-start(f32[384]{0:T(512)} %param.18) | copy-start | bytes 4612
  317.0 7.6 %copy-start.5 = (f32[1,8,384]{2,0,1:T(1,128)}, f32[1,8,384]{2,0,1:T(1,128)S(1)}, u32[]{:S(2)}) copy-start(f32[1,8,384]{2,0,1:T(1,128)S(1)} %get-tuple-element.34) | copy-start | bytes 36868
  317.0 7.6 %copy-start.6 = (f32[1,8,384]{2,0,1:T(1,128)}, f32[1,8,384]{2,0,1:T(1,128)S(1)}, u32[]{:S(2)}) copy-start(f32[1,8,384]{2,0,1:T(1,128)S(1)} %get-tuple-element.35) | copy-start | bytes 36868
  317.8 6.8 %copy-start.8 = (f32[384]{0:T(512)}, f32[384]{0:T(512)S(1)}, u32[]{:S(2)}) copy-start(f32[384]{0:T(512)S(1)} %get-tuple-element.28) | copy-start | bytes 4612
  317.8 6.8 %copy-start.9 = (f32[384]{0:T(512)}, f32[384]{0:T(512)S(1)}, u32[]{:S(2)}) copy-start(f32[384]{0:T(512)S(1)} %get-tuple-element.29) | copy-start | bytes 4612
  319.0 5.6 %copy-start.4 = (bf16[384,3072]{1,0:T(8,128)(2,1)S(1)}, bf16[384,3072]{1,0:T(8,128)(2,1)}, u32[]{:S(2)}) copy-start(bf16[384,3072]{1,0:T(8,128)(2,1)} %get-tuple-element.19) | copy-start | bytes 7077892
  324.6 3.8 %copy-start.1 = (bf16[512,3072]{1,0:T(8,128)(2,1)S(1)}, bf16[512,3072]{1,0:T(8,128)(2,1)}, u32[]{:S(2)}) copy-start(bf16[512,3072]{1,0:T(8,128)(2,1)} %param.10) | copy-start | bytes 9437188

commit v3 on v2

--- a/solution.py
+++ b/solution.py
@@ -154,7 +154,8 @@
     along = [[post(k, own_rows(k), me, col, (other, col)) for other in far] for k in range(2)]
     over = [[post(k, own_rows(k), me, col, (beside, col))] for k in range(2)]
     mat_sent = []
-    for k in range(2):
+
+    def post_mats(k):
         for shift in range(1, n):
             other = others[shift - 1]
             copy = send(
@@ -166,6 +167,8 @@
             )
             copy.start()
             mat_sent.append(copy)
+
+    post_mats(0)
     for load in loads:
         load.start()
     for load, store in zip(loads, stores):
@@ -183,6 +186,7 @@
             over[k].append(post(k, held(k, owner, col), owner, col, (beside, col)))
             crossed[k].append((owner, post(k, held(k, owner, col), owner, col, (me, across))))
             shared[k].append(post(k, held(k, owner, col), owner, col, (me, core)))
+    post_mats(1)
     for k in range(2):
         for copy, owner in zip(over[k], [beside] + [flipped(owner) for owner in from_far]):
             copy.wait_recv()
@@ -413,8 +417,8 @@
     hidden_act = act_value.astype(jnp.bfloat16)
     act_grad = jnp.dot(out_grad_all, cut_down, preferred_element_type=jnp.float32)
     pre_grad = pull_back(act_grad)[0].astype(jnp.bfloat16)
-    grad_down = contract_tokens(out_grad_all, hidden_act)
-    grad_up = contract_tokens(normed_all, pre_grad)
+    grad_down = lax.optimization_barrier(contract_tokens(out_grad_all, hidden_act))
+    grad_up = lax.optimization_barrier(contract_tokens(normed_all, pre_grad))
     rowpart_up, spent_up, col_part_up = column_block(grad_up, col_up, depth)
     rowpart_down, spent_down, col_part_down = column_block(grad_down, col_down, depth)
     by_row = jnp.stack([rowpart_up, rowpart_down, spent_up, spent_down]).reshape(4, n, rows)

time: 329 us -> 315 us (0.957)
  matrix products: 30.6 us -> 17.2 us
  local copies, waits for them, and re-layouts: 16.2 us -> 9.27 us
  other arithmetic: 27.9 us -> 34.3 us
    dot_general x2, matrix products: 22.4 us -> 7.25 us  [contract_tokens(): lax.dot_general(left, right, (((0,), (0,)), ((), ())), preferred_element_...]
    dot_general x2 -> x0, local copies, waits for them, and re-layouts: 9.76 us -> none  [contract_tokens(): lax.dot_general(left, right, (((0,), (0,)), ((), ())), preferred_element_...]
    reduce_sum x2, other arithmetic: 4.2 us -> 9.46 us  [column_block(): spent = jnp.sum(grad * grad * (1.0 / col_new)[None, :], axis=1)]
    dot_general x0 -> x1, matrix products: none -> 3.4 us  [exchanged_step(): jnp.dot(out_grad_all, cut_down, preferred_element_type=jnp.float32)]
where the time goes in v3:
time: 315 us; the launch traced here: 314 us
  Pallas kernels  253 us (80%)
  other arithmetic  34.3 us (11%)
  matrix products  17.2 us (5%)
  local copies, waits for them, and re-layouts  9.27 us (3%)
    pallas_call x1, Pallas kernels, returned(): pl.pallas_call(functools.partial(return_kernel, n, breadth), out_shape=(j...  127 us
    pallas_call x1, Pallas kernels, spread(): pl.pallas_call(functools.partial(spread_kernel, n), out_shape=(jax.ShapeD...  126 us
    reduce_sum x2, other arithmetic, column_block(): spent = jnp.sum(grad * grad * (1.0 / col_new)[None, :], axis=1)  9.46 us
    dot_general x2, matrix products, contract_tokens(): lax.dot_general(left, right, (((0,), (0,)), ((), ())), preferred_element_...  7.25 us
    dot_general x1, matrix products, exchanged_step(): pre_act = jnp.dot(normed_all, cut_up, preferred_element_type=jnp.float32)  6.54 us

profile of v3, /device:TPU:0, one launch (start us, length us, event | category | flops | bytes accessed | tf_op | source)
XLA Modules:
  0.0 314.5 jit_solution(14913980683831899789)
XLA Ops:
  0.6 0.8 compare_select_fusion
  1.5 1.1 copy-done
  2.5 1.9 gather_fusion
  4.5 1.4 convert_reduce_fusion
  5.9 1.5 fusion.2
  7.5 2.4 fusion.4.act_a
  9.9 4.2 %convert_element_type.32.mat_a = bf16[384,3072]{1,0:T(8,128)(2,1)} convert(f32[384,3072]{1,0:T(8,128)} %param.14) | non-fusion elementwise | flops 1179648 | bytes 7077888 | tf_op jit(solution)/shard_map/convert_element_type | solution.py:459
  14.2 1.7 convert_element_type.33.mat_b
  15.9 125.8 %shard_map.145 = (bf16[1024,3072]{1,0:T(8,128)(2,1)}, bf16[1024,3072]{1,0:T(8,128)(2,1)}, bf16[3072,384]{1,0:T(8,128)(2,1)}, bf16[3072,384]{1,0:T(8,128)(2,1)}) custom-call(bf16[128,3072]{1,0:T(8,128)(2,1)} %fusion.4.act_a, bf16[128,3072]{1,0:T(8,128)(2,1)} %act_b.1, bf16[384,3072]{1,0:T(8,128)(2,1)} %convert_element_type.32.mat_a, ...), custom_call_target="tpu_custom_call" | custom-call | tf_op jit(solution)/shard_map/pallas_call | solution.py:216
  141.7 6.5 %fusion.38 = f32[1024,384]{1,0:T(8,128)S(1)} fusion(bf16[1024,3072]{1,0:T(8,128)(2,1)} %get-tuple-element.15, bf16[3072,384]{1,0:T(8,128)(2,1)} %get-tuple-element.18), kind=kOutput, calls=%fused_computation.67 | convolution fusion | flops 2415919104 | bytes 10223616 | tf_op jit(solution)/shard_map/dot_general | solution.py:415
  148.3 3.4 %fusion.37 = f32[1024,384]{1,0:T(8,128)S(1)} fusion(bf16[1024,3072]{1,0:T(8,128)(2,1)S(1)} %copy-done.14, bf16[3072,384]{1,0:T(8,128)(2,1)S(1)} %copy-done.15), kind=kOutput, calls=%fused_computation.66 | convolution fusion | flops 2415919104 | bytes 10223616 | tf_op jit(solution)/shard_map/dot_general | solution.py:418
  151.8 3.7 %fusion.13 = f32[3072,384]{1,0:T(8,128)S(1)} fusion(bf16[1024,3072]{1,0:T(8,128)(2,1)S(1)} %bitcast.27, f32[1024,384]{1,0:T(8,128)S(1)} %fusion.38, f32[1024,384]{1,0:T(8,128)S(1)} %fusion.37), kind=kOutput, calls=%fused_computation.27 | convolution fusion | flops 2423783424 | bytes 14155776 | tf_op jit(solution)/shard_map/dot_general | solution.py:26
  156.1 1.6 copy-done.2
  157.7 3.6 %fusion.12 = f32[3072,384]{1,0:T(8,128)S(1)} fusion(bf16[1024,3072]{1,0:T(8,128)(2,1)S(1)} %copy-done.14, f32[1024,384]{1,0:T(8,128)S(1)} %fusion.38), kind=kOutput, calls=%fused_computation.26 | convolution fusion | flops 2419458048 | bytes 12582912 | tf_op jit(solution)/shard_map/dot_general | solution.py:26
  161.8 1.6 copy-done.4
  163.4 0.8 broadcast_divide_fusion
  164.2 6.8 %multiply_reduce_fusion = (f32[3072]{0:T(1024)S(1)}, f32[3072]{0:T(1024)S(1)}, bf16[3072,384]{1,0:T(8,128)(2,1)}) fusion(f32[3072,384]{1,0:T(8,128)} %copy-done.4, f32[384]{0:T(512)S(1)} %get-tuple-element.30), kind=kLoop, calls=%fused_computation.3 | loop fusion | flops 7071744 | bytes 7104000 | tf_op jit(solution)/shard_map/reduce_sum | solution.py:405
  171.1 2.6 multiply_reduce_fusion.1
  173.7 0.8 concatenate.5
  175.1 127.0 %shard_map.146 = (bf16[384,3072]{1,0:T(8,128)(2,1)}, bf16[384,3072]{1,0:T(8,128)(2,1)}, f32[8,8,384]{2,1,0:T(8,128)}, f32[2,384]{1,0:T(2,128)}, f32[2,128]{1,0:T(2,128)}) custom-call(bf16[3072,384]{1,0:T(8,128)(2,1)} %get-tuple-element.35.mat_a, bf16[3072,384]{1,0:T(8,128)(2,1)} %get-tuple-element.34.mat_b, f32[8,8,384]{2,1,0:T(8,128)} %bitcast.17, ...), custom_call_target="tpu_custom_call" | custom-call | tf_op jit(solution)/shard_map/pallas_call | solution.py:356
  302.1 0.9 slice_bitcast_fusion
  303.1 0.8 slice_reduce_fusion
  305.1 5.5 %multiply_divide_fusion = f32[384,3072]{1,0:T(8,128)} fusion(bf16[384,3072]{1,0:T(8,128)(2,1)} %get-tuple-element.23, f32[]{:T(128)} %bitcast.9, f32[3072]{0:T(1024)S(1)} %bitcast.22, f32[384]{0:T(512)S(1)} %get-tuple-element.28), kind=kLoop, calls=%fused_computation.1 | loop fusion | flops 4718592 | bytes 7091716 | tf_op jit(solution)/shard_map/div | solution.py:437
  310.7 3.8 %multiply_divide_fusion.1 = f32[384,3072]{1,0:T(8,128)} fusion(bf16[384,3072]{1,0:T(8,128)(2,1)S(1)} %copy-done.6, f32[]{:T(128)} %bitcast.7, f32[3072]{0:T(1024)S(1)} %bitcast.24, f32[384]{0:T(512)S(1)} %get-tuple-element.29), kind=kLoop, calls=%fused_computation.2 | loop fusion | flops 4718592 | bytes 7091716 | tf_op jit(solution)/shard_map/div | solution.py:436
  (53 shorter events, 3.1 us)
Async XLA Ops:
  0.6 1.9 copy-start
  2.5 1.9 copy-start.16
  2.5 4.9 %copy-start.9 = (f32[3072]{0:T(1024)S(1)}, f32[3072]{0:T(1024)}, u32[]{:S(2)}) copy-start(f32[3072]{0:T(1024)} %param.13) | copy-start | bytes 36868
  9.9 4.2 %copy-start.5 = (f32[384,3072]{1,0:T(8,128)S(1)}, f32[384,3072]{1,0:T(8,128)}, u32[]{:S(2)}) copy-start(f32[384,3072]{1,0:T(8,128)} %param.15) | copy-start | bytes 14155780
  141.7 6.6 %copy-start.14 = (bf16[1024,3072]{1,0:T(8,128)(2,1)S(1)}, bf16[1024,3072]{1,0:T(8,128)(2,1)}, u32[]{:S(2)}) copy-start(bf16[1024,3072]{1,0:T(8,128)(2,1)} %get-tuple-element.16) | copy-start | bytes 18874372
  141.7 6.6 %copy-start.15 = (bf16[3072,384]{1,0:T(8,128)(2,1)S(1)}, bf16[3072,384]{1,0:T(8,128)(2,1)}, u32[]{:S(2)}) copy-start(bf16[3072,384]{1,0:T(8,128)(2,1)} %get-tuple-element.17) | copy-start | bytes 7077892
  141.7 10.0 %slice-start = ((s8[6291456]{0:T(1024)(128)(4,1)}), s8[4194304]{0:T(1024)(128)(4,1)S(1)}, s32[]{:S(2)}) async-start(s8[6291456]{0:T(1024)(128)(4,1)} %bitcast.26), calls=%async_computation | async-start | bytes 8388608
  148.3 3.4 %slice-start.1 = ((s8[6291456]{0:T(1024)(128)(4,1)}), s8[2097152]{0:T(1024)(128)(4,1)S(1)}, s32[]{:S(2)}) async-start(s8[6291456]{0:T(1024)(128)(4,1)} %bitcast.26), calls=%async_computation.1 | async-start | bytes 4194304
  155.5 2.2 copy-start.2
  161.2 2.2 copy-start.4
  164.2 6.8 %copy-start.3 = (f32[3072,384]{1,0:T(8,128)S(1)}, f32[3072,384]{1,0:T(8,128)}, u32[]{:S(2)}) copy-start(f32[3072,384]{1,0:T(8,128)} %copy-done.2) | copy-start | bytes 14155780
  171.1 3.4 %copy-start.12 = (f32[384]{0:T(512)S(1)}, f32[384]{0:T(512)}, u32[]{:S(2)}) copy-start(f32[384]{0:T(512)} %param.16) | copy-start | bytes 4612
  171.1 3.4 %copy-start.13 = (f32[384]{0:T(512)S(1)}, f32[384]{0:T(512)}, u32[]{:S(2)}) copy-start(f32[384]{0:T(512)} %param.18) | copy-start | bytes 4612
  303.1 7.6 %copy-start.7 = (f32[1,8,384]{2,0,1:T(1,128)}, f32[1,8,384]{2,0,1:T(1,128)S(1)}, u32[]{:S(2)}) copy-start(f32[1,8,384]{2,0,1:T(1,128)S(1)} %get-tuple-element.36) | copy-start | bytes 36868
  303.1 7.6 %copy-start.8 = (f32[1,8,384]{2,0,1:T(1,128)}, f32[1,8,384]{2,0,1:T(1,128)S(1)}, u32[]{:S(2)}) copy-start(f32[1,8,384]{2,0,1:T(1,128)S(1)} %get-tuple-element.37) | copy-start | bytes 36868
  303.9 6.8 %copy-start.10 = (f32[384]{0:T(512)}, f32[384]{0:T(512)S(1)}, u32[]{:S(2)}) copy-start(f32[384]{0:T(512)S(1)} %get-tuple-element.28) | copy-start | bytes 4612
  303.9 6.8 %copy-start.11 = (f32[384]{0:T(512)}, f32[384]{0:T(512)S(1)}, u32[]{:S(2)}) copy-start(f32[384]{0:T(512)S(1)} %get-tuple-element.29) | copy-start | bytes 4612
  305.1 5.6 %copy-start.6 = (bf16[384,3072]{1,0:T(8,128)(2,1)S(1)}, bf16[384,3072]{1,0:T(8,128)(2,1)}, u32[]{:S(2)}) copy-start(bf16[384,3072]{1,0:T(8,128)(2,1)} %get-tuple-element.19) | copy-start | bytes 7077892
  310.7 3.8 %copy-start.1 = (bf16[512,3072]{1,0:T(8,128)(2,1)S(1)}, bf16[512,3072]{1,0:T(8,128)(2,1)}, u32[]{:S(2)}) copy-start(bf16[512,3072]{1,0:T(8,128)(2,1)} %param.10) | copy-start | bytes 9437188
